TPU v7x, 128 devices: a whole 4x4x4 slice. The times are simulated.
128 devices in a mesh: group: 8 (over z, core), pair: 16 (over y, x).
Axes of the slice: x: 4, y: 4, z: 4, core: 2. Of those that a mesh axis runs over, the one named last changes fastest.
Arguments:
- query_embed: bfloat16 [8, 16, 1024], P('group'), may hold values from -6 to 6
- teacher_scores: float32 [8, 16, 16, 32], P('group', 'pair'), may hold values from -9 to 9
- pair_owner: int32 [8, 16, 16, 32, 1], P('group', 'pair'), may hold values from 0 to 127; in each aligned block of 512 rows (0 to 511, 512 to 1023, ..., all dimensions but the last counted through in order) at most 8 rows name the same one
- pair_row: int32 [8, 16, 16, 32], P('group', 'pair'), may hold values from 0 to 2047
- passage_hidden: bfloat16 [262144, 1024], P(('group', 'pair')), may hold values from -24 to 24
- projection: bfloat16 [1024, 1024], replicated, may hold values from -0.1875 to 0.1875
Outputs:
- query_loss: float32 [8, 16], P('group', 'pair')
- query_grad: float32 [8, 16, 1024], P('group', 'pair')
- hidden_grad: bfloat16 [262144, 1024], P(('group', 'pair'))
- projection_grad: float32 [1024, 1024], P(('group', 'pair'))
Inputs may be any that keep to these rules, and one draw needn't show every extreme that they name: `pair_owner`: owners are numbered with group as the slower index. Among the 512 candidates held by one device, at most 8 name the same owner, and every draw has a device and an owner with exactly 8. `pair_row`: A passage may be named by several candidates.
All inputs are finite; a program needn't handle non-finite values.
Results may differ from a plain program's by a relative error of at most 0.022.
Values may be sent and summed in bfloat16 or wider, within the bound.
A program may use at most 128 MiB of HBM per device.

v0:
```python
import math
import jax
import jax.numpy as jnp
from jax import lax
from jax.sharding import PartitionSpec as P

loss_scale = 1024.0


def soft_steps(values_all, values_own):
    return jax.nn.sigmoid((values_all[:, None, :] - values_own[:, :, None]) * 2.0)


def score_slope(soft_step, grad_all, grad_own):
    slopes = soft_step * (1.0 - soft_step)
    return 2.0 * (jnp.sum(slopes * grad_all[:, None, :], -1) - grad_own * jnp.sum(slopes, -1))


def shards(query_embed, teacher_scores, pair_owner, pair_row, passage_hidden, projection):
    model_width = query_embed.shape[2]
    query_rows = query_embed.shape[1]
    cand_dev = teacher_scores.shape[3]
    pass_rows = passage_hidden.shape[0]
    pair_size = lax.axis_size("pair")
    group_size = lax.axis_size("group")
    devices = pair_size * group_size
    cand_all = cand_dev * pair_size
    pair_count = query_rows * cand_dev
    capacity = max(2, 2 * pair_count // devices)
    query_dev = query_rows // pair_size
    inv_root = 1.0 / math.sqrt(model_width)
    spearman_den = float(cand_all * (cand_all * cand_all - 1))
    embedded = jnp.dot(passage_hidden, projection, preferred_element_type=jnp.float32).astype(
        jnp.bfloat16
    )
    owner_dev = pair_owner.reshape(pair_count)
    row_index = pair_row.reshape(pair_count)
    owner_marks = (owner_dev[:, None] == jnp.arange(devices, dtype=jnp.int32)[None, :]).astype(
        jnp.int32
    )
    slot_index = jnp.sum(jnp.cumsum(owner_marks, axis=0) * owner_marks, axis=1) - 1
    requests = jnp.zeros((devices, capacity), jnp.int32).at[owner_dev, slot_index].set(row_index)
    queries = query_embed[0]
    asked_rows = lax.all_to_all(
        requests, ("group", "pair"), split_axis=0, concat_axis=0, tiled=True
    )
    vectors = jnp.take(embedded, asked_rows, axis=0)
    replies = lax.all_to_all(vectors, ("group", "pair"), split_axis=0, concat_axis=0, tiled=True)
    pair_vectors = replies[owner_dev, slot_index].reshape(query_rows, cand_dev, model_width)
    scores = (
        jnp.einsum("qd,qcd->qc", queries, pair_vectors, preferred_element_type=jnp.float32)
        * inv_root
    )
    teacher_own = teacher_scores.reshape(query_rows, cand_dev)
    scores_all, teacher_all = (
        lax.all_gather(scores, "pair", axis=1, tiled=True),
        lax.all_gather(teacher_own, "pair", axis=1, tiled=True),
    )
    soft_step = soft_steps(scores_all, scores)
    rank_student = 0.5 + jnp.sum(soft_step, -1)
    rank_teacher = 0.5 + jnp.sum(soft_steps(teacher_all, teacher_own), -1)
    rank_gap = rank_student - rank_teacher
    loss_part = 6.0 * jnp.sum(rank_gap * rank_gap, axis=1) / spearman_den
    rank_grad = loss_scale * 12.0 * rank_gap / spearman_den
    grad_all = lax.all_gather(rank_grad, "pair", axis=1, tiled=True)
    score_grad = score_slope(soft_step, grad_all, rank_grad)
    query_part = (
        jnp.sum(score_grad[:, :, None] * pair_vectors.astype(jnp.float32), axis=1) * inv_root
    )
    pair_grad = (
        score_grad[:, :, None] * queries.astype(jnp.float32)[:, None, :] * inv_root
    ).astype(jnp.bfloat16)
    query_sum, loss_own = (
        lax.psum_scatter(
            query_part.astype(jnp.bfloat16), "pair", scatter_dimension=0, tiled=True
        ).astype(jnp.float32),
        lax.psum_scatter(
            loss_part.astype(jnp.bfloat16), "pair", scatter_dimension=0, tiled=True
        ).astype(jnp.float32),
    )
    outgoing = (
        jnp.zeros((devices, capacity, model_width), jnp.bfloat16)
        .at[owner_dev, slot_index]
        .set(pair_grad.reshape(pair_count, model_width))
    )
    arrived = lax.all_to_all(outgoing, ("group", "pair"), split_axis=0, concat_axis=0, tiled=True)
    embed_grad = (
        jnp.zeros((pass_rows, model_width), jnp.float32)
        .at[asked_rows.reshape(-1)]
        .add(arrived.reshape(-1, model_width).astype(jnp.float32))
    )
    grad_rounded = embed_grad.astype(jnp.bfloat16)
    hidden_grad = jnp.einsum(
        "pe,de->pd", grad_rounded, projection, preferred_element_type=jnp.float32
    ).astype(jnp.bfloat16)
    projection_grad = lax.psum_scatter(
        jnp.einsum("pr,pe->re", passage_hidden, grad_rounded, preferred_element_type=jnp.float32),
        ("group", "pair"),
        scatter_dimension=0,
        tiled=True,
    )
    return (
        loss_own.reshape(1, query_dev),
        query_sum.reshape(1, query_dev, model_width),
        hidden_grad,
        projection_grad,
    )


def solution(mesh):
    placed = (
        P("group", None, None),
        P("group", "pair", None, None),
        P("group", "pair", None, None, None),
        P("group", "pair", None, None),
        P(("group", "pair"), None),
        P(),
    )
    return jax.shard_map(
        shards,
        mesh=mesh,
        in_specs=placed,
        out_specs=(
            P("group", "pair"),
            P("group", "pair", None),
            P(("group", "pair"), None),
            P(("group", "pair"), None),
        ),
        check_vma=False,
    )
```

profile of v0, /device:TPU:0, one launch (start us, length us, event | category | flops | bytes accessed | tf_op | source)
XLA Modules:
  0.0 964.4 jit_solution(8039499689911197415)
XLA Ops:
  10.2 1.4 reduce.10
  12.3 22.0 %scatter_fusion = s32[128,8]{0,1:T(8,128)S(1)} fusion(s32[128,8]{0,1:T(8,128)S(1)} %broadcast_in_dim.18, s32[512]{0:T(512)S(1)} %bitcast.82, s32[512]{0:T(512)S(1)} %reshape.243), kind=kCustom, calls=%fused_computation.2 | custom fusion | bytes 10240 | tf_op jit(solution)/shard_map/scatter | solution.py:42
  35.0 11.1 %all-to-all-start = ((s32[128,1,8]{2,1,0:T(1,128)}), s32[128,1,8]{2,1,0:T(1,128)S(1)}, u32[]{:S(2)}, u32[]{:S(2)}) async-start(s32[128,1,8]{2,1,0:T(1,128)} %copy.31), calls=%async_computation | async-start | bytes 131072 | tf_op jit(solution)/shard_map/all_to_all | solution.py:44
  46.2 8.3 convolution_convert_fusion.1
  56.0 8.8 gather_fusion
  64.7 3.2 bitcast_select_fusion
  67.9 9.1 all-to-all-start.1
  77.1 41.4 %all-gather = f32[1,1,16,512]{2,1,0,3:T(1,128)S(1)} all-gather(f32[1,1,16,32]{2,1,0,3:T(1,128)S(1)} %copy.35), channel_id=2, replica_groups=mesh['group'=8,'pair'=16] {'pair'}, dimensions={3}, use_global_device_ids=true | all-gather | bytes 34816 | tf_op jit(solution)/shard_map/all_gather | solution.py:57
  119.1 7.7 gather_fusion.1
  127.2 22.0 %all-gather.1 = f32[16,32,16]{1,2,0:T(8,128)S(1)} all-gather(f32[1,32,16]{1,2,0:T(8,128)S(1)} %get-tuple-element.28), channel_id=1, replica_groups=mesh['group'=8,'pair'=16] {'pair'}, dimensions={0}, use_global_device_ids=true | all-gather | bytes 34816 | tf_op jit(solution)/shard_map/all_gather | solution.py:56
  149.9 22.6 %all-gather.2 = f32[16,32,16]{1,2,0:T(8,128)S(1)} all-gather(f32[1,32,16]{1,2,0:T(8,128)S(1)} %multiply_bitcast_fusion), channel_id=1, replica_groups=mesh['group'=8,'pair'=16] {'pair'}, dimensions={0}, use_global_device_ids=true | all-gather | bytes 34816 | tf_op jit(solution)/shard_map/all_gather | solution.py:65
  173.4 1.2 fusion.5
  174.7 1.6 broadcast_in_dim.23
  176.2 73.0 %scatter_fusion.1 = bf16[128,8,1024]{2,1,0:T(8,128)(2,1)} fusion(bf16[128,8,1024]{2,1,0:T(8,128)(2,1)} %broadcast_in_dim.23, s32[512]{0:T(512)S(1)} %bitcast.83, bf16[512,1024]{1,0:T(8,128)(2,1)} %fusion.5), kind=kCustom, calls=%fused_computation.3 | custom fusion | bytes 3149824 | tf_op jit(solution)/shard_map/scatter | solution.py:84
  249.2 8.3 all-to-all-start.2
  258.5 28.3 %all-to-all-done.2 = bf16[128,8,1024]{2,1,0:T(8,128)(2,1)} async-done(((bf16[128,8,1024]{2,1,0:T(8,128)(2,1)}), bf16[128,8,1024]{2,1,0:T(8,128)(2,1)}, u32[]{:S(2)}, u32[]{:S(2)}) %all-to-all-start.2) | async-done | bytes 2097184 | tf_op jit(solution)/shard_map/all_to_all | solution.py:86
  286.8 13.4 %scatter_custom_fusion.2 = f32[2048,1024]{1,0:T(8,128)} fusion(s32[1024]{0:T(1024)S(1)} %bitcast.101, f32[]{:T(128)} %constant.26.clone.1, bf16[128,8,1024]{2,1,0:T(8,128)(2,1)} %all-to-all-done.2), kind=kCustom, calls=%fused_computation.5 | custom fusion | flops 2097152 | bytes 10485764 | tf_op jit(solution)/shard_map/scatter-add | solution.py:90
  300.2 11.2 %convolution_bitcast_fusion = f32[1024,1024]{0,1:T(8,128)} fusion(bf16[2048,1024]{1,0:T(8,128)(2,1)} %param.10, f32[2048,1024]{1,0:T(8,128)} %scatter_custom_fusion.2), kind=kOutput, calls=%fused_computation.10 | convolution fusion | flops 4297064448 | bytes 16777216 | tf_op jit(solution)/shard_map/pr,pe->re/dot_general | solution.py:97
  311.3 5.3 copy.41
  317.9 72.1 %all-reduce.2 = (bf16[16]{0:T(256)(128)(2,1)S(1)}, bf16[16,1024]{1,0:T(8,128)(2,1)S(1)}) all-reduce(bf16[16]{0:T(256)(128)(2,1)S(1)} %multiply_convert_fusion.1, bf16[16,1024]{1,0:T(8,128)(2,1)S(1)} %multiply_convert_fusion), channel_id=3, replica_groups=mesh['group'=8,'pair'=16] {'pair'}, use_global_device_ids=true, to_apply=%region_7.8.clone | all-reduce | flops 16400 | bytes 65600
  390.0 1.2 dynamic-slice.1
  391.9 1.2 bitcast_convert_fusion.1
  393.2 9.5 convolution_convert_fusion
  402.6 553.7 %reduce-scatter.4.cloned.1.call-done = f32[8,1024]{1,0:T(8,128)} async-done(((f32[1024,1024]{1,0:T(8,128)}), f32[8,1024]{1,0:T(8,128)}) %reduce-scatter.4.cloned.1.call-update) | async-done | bytes 32784
  (58 shorter events, 10.7 us)
Async XLA Ops:
  7.2 39.0 %copy-start = (bf16[1024,1024]{1,0:T(8,128)(2,1)S(1)}, bf16[1024,1024]{1,0:T(8,128)(2,1)}, u32[]{:S(2)}) copy-start(bf16[1024,1024]{1,0:T(8,128)(2,1)} %param.11) | copy-start | bytes 6291460
  35.0 20.6 %all-to-all-start = ((s32[128,1,8]{2,1,0:T(1,128)}), s32[128,1,8]{2,1,0:T(1,128)S(1)}, u32[]{:S(2)}, u32[]{:S(2)}) async-start(s32[128,1,8]{2,1,0:T(1,128)} %copy.31), calls=%async_computation | async-start | bytes 131072 | tf_op jit(solution)/shard_map/all_to_all | solution.py:44
  64.7 12.3 %copy-start.2 = (f32[1,1,16,32]{3,2,1,0:T(8,128)S(1)}, f32[1,1,16,32]{3,2,1,0:T(8,128)}, u32[]{:S(2)}) copy-start(f32[1,1,16,32]{3,2,1,0:T(8,128)} %param.7) | copy-start | bytes 6148
  64.7 53.9 %copy-start.1 = (bf16[1,16,1024]{2,1,0:T(8,128)(2,1)S(1)}, bf16[1,16,1024]{2,1,0:T(8,128)(2,1)}, u32[]{:S(2)}) copy-start(bf16[1,16,1024]{2,1,0:T(8,128)(2,1)} %param.6) | copy-start | bytes 98308
  67.9 51.1 %all-to-all-start.1 = ((bf16[128,8,1024]{2,1,0:T(8,128)(2,1)}), bf16[128,8,1024]{2,1,0:T(8,128)(2,1)}, u32[]{:S(2)}, u32[]{:S(2)}) async-start(bf16[128,8,1024]{2,1,0:T(8,128)(2,1)} %bitcast_select_fusion), calls=%async_computation.1 | async-start | bytes 4194304 | tf_op jit(solution)/shard_map/all_to_all | solution.py:48
  249.2 37.6 %all-to-all-start.2 = ((bf16[128,8,1024]{2,1,0:T(8,128)(2,1)}), bf16[128,8,1024]{2,1,0:T(8,128)(2,1)}, u32[]{:S(2)}, u32[]{:S(2)}) async-start(bf16[128,8,1024]{2,1,0:T(8,128)(2,1)} %scatter_fusion.1), calls=%async_computation.2 | async-start | bytes 4194304 | tf_op jit(solution)/shard_map/all_to_all | solution.py:86
  257.5 698.9 %reduce-scatter.4.cloned.1.call-start = ((), (), s32[]{:S(2)}) async-start(), calls=%async_computation.4 | async-start | bytes 4227072
  316.7 0.7 copy-start.3
Sparse Core Ops, SparseCore 0:
  316.8 639.5 reduce-scatter.3
where the time goes:
time: 968 us; the launch traced here: 964 us
  waiting for transfers between devices  583 us (60%)
  blocking collectives  158 us (16%)
  local copies, waits for them, and re-layouts  125 us (13%)
  matrix products  29.3 us (3%)
  starting transfers between devices  28.6 us (3%)
  other arithmetic  24 us (2%)
  between operations  16.1 us (2%)
    unnamed x2, waiting for transfers between devices  554 us
    scatter x1, local copies, waits for them, and re-layouts, shards(): outgoing = jnp.zeros((devices, capacity, model_width), jnp.bfloat16).at[o...  73 us
    unnamed x1, blocking collectives  72.1 us
    all_gather x1, blocking collectives, shards(): lax.all_gather(teacher_own, 'pair', axis=1, tiled=True)  41.4 us
    all_to_all x1, waiting for transfers between devices, shards(): lax.all_to_all(outgoing, ('group', 'pair'), split_axis=0, concat_axis=0,...  28.3 us
    all_gather x1, blocking collectives, shards(): grad_all = lax.all_gather(rank_grad, 'pair', axis=1, tiled=True)  22.6 us
    all_gather x1, blocking collectives, shards(): lax.all_gather(scores, 'pair', axis=1, tiled=True)  22 us
    scatter x1, local copies, waits for them, and re-layouts, shards(): jnp.zeros((devices, capacity), jnp.int32).at[owner_dev, slot_index]  22 us
  transfers between devices with their start and end apart: 4, of which 3 were waited for; matrix products, arithmetic and copies ran while one was open for 2% of the time, Pallas kernels for 0%

commit v1 on v0

--- a/solution.py
+++ b/solution.py
@@ -5,6 +5,27 @@
 from jax.sharding import PartitionSpec as P
 
 loss_scale = 1024.0
+
+
+def gather_around(value, axis, dim):
+    devices, place, rows = (lax.axis_size(axis), lax.axis_index(axis), value.shape[dim])
+    right = [(i, (i + 1) % devices) for i in range(devices)]
+    left = [(i, (i - 1) % devices) for i in range(devices)]
+    result = jnp.zeros((*value.shape[:dim], devices * rows, *value.shape[dim + 1 :]), value.dtype)
+    result = lax.dynamic_update_slice_in_dim(result, value, place * rows, axis=dim)
+    from_left = from_right = value
+    halfway = devices // 2
+    for lap in range(1, halfway + 1):
+        from_left = lax.ppermute(from_left, axis, right)
+        result = lax.dynamic_update_slice_in_dim(
+            result, from_left, (place - lap) % devices * rows, axis=dim
+        )
+        if lap < devices - halfway:
+            from_right = lax.ppermute(from_right, axis, left)
+            result = lax.dynamic_update_slice_in_dim(
+                result, from_right, (place + lap) % devices * rows, axis=dim
+            )
+    return result
 
 
 def soft_steps(values_all, values_own):
@@ -54,7 +75,7 @@
     teacher_own = teacher_scores.reshape(query_rows, cand_dev)
     scores_all, teacher_all = (
         lax.all_gather(scores, "pair", axis=1, tiled=True),
-        lax.all_gather(teacher_own, "pair", axis=1, tiled=True),
+        gather_around(teacher_own, "pair", 1),
     )
     soft_step = soft_steps(scores_all, scores)
     rank_student = 0.5 + jnp.sum(soft_step, -1)

time: 968 us -> 1000 us (1.033)
  blocking collectives: 158 us -> 117 us
  starting transfers between devices: 28.6 us -> 65 us
  waiting for transfers between devices: 583 us -> 618 us
    all_gather x1 -> x0, blocking collectives: 41.4 us -> none  [shards(): lax.all_gather(teacher_own, 'pair', axis=1, tiled=True)]
    ppermute x0 -> x15, starting transfers between devices: none -> 36.5 us  [the longest x7 36.4 us: gather_around(): from_right = lax.ppermute(from_right, axis, left)]
    ppermute x0 -> x15, waiting for transfers between devices: none -> 34.3 us  [the longest x8 34.3 us: gather_around(): from_left = lax.ppermute(from_left, axis, right)]
  transfers between devices with their start and end apart: 4 -> 19, of which waited for: 3 -> 11; matrix products, arithmetic and copies ran while one was open for 2% -> 3% of each run, Pallas kernels for 0% -> 0%
where the time goes in v1:
time: 1000 us; the launch traced here: 998 us
  waiting for transfers between devices  618 us (62%)
  local copies, waits for them, and re-layouts  130 us (13%)
  blocking collectives  117 us (12%)
  starting transfers between devices  65 us (6%)
  matrix products  29.3 us (3%)
  other arithmetic  24 us (2%)
  between operations  16.1 us (2%)
    unnamed x2, waiting for transfers between devices  554 us
    scatter x1, local copies, waits for them, and re-layouts, shards(): outgoing = jnp.zeros((devices, capacity, model_width), jnp.bfloat16).at[o...  73 us
    unnamed x1, blocking collectives  72.1 us
    ppermute x7, starting transfers between devices, gather_around(): from_right = lax.ppermute(from_right, axis, left)  36.4 us
    ppermute x8, waiting for transfers between devices, gather_around(): from_left = lax.ppermute(from_left, axis, right)  34.3 us
    all_to_all x1, waiting for transfers between devices, shards(): lax.all_to_all(outgoing, ('group', 'pair'), split_axis=0, concat_axis=0,...  28.1 us
    all_gather x1, blocking collectives, shards(): grad_all = lax.all_gather(rank_grad, 'pair', axis=1, tiled=True)  23.8 us
    scatter x1, local copies, waits for them, and re-layouts, shards(): jnp.zeros((devices, capacity), jnp.int32).at[owner_dev, slot_index]  22 us
  transfers between devices with their start and end apart: 19, of which 11 were waited for; matrix products, arithmetic and copies ran while one was open for 3% of the time, Pallas kernels for 0%

profile of v1, /device:TPU:0, one launch (start us, length us, event | category | flops | bytes accessed | tf_op | source)
XLA Modules:
  0.0 998.4 jit_solution(12052369414304187016)
XLA Ops:
  12.3 22.0 %scatter_fusion = s32[128,8]{0,1:T(8,128)S(1)} fusion(s32[128,8]{0,1:T(8,128)S(1)} %broadcast_in_dim.18, s32[512]{0:T(512)S(1)} %bitcast.81, s32[512]{0:T(512)S(1)} %reshape.320), kind=kCustom, calls=%fused_computation.2 | custom fusion | bytes 10240 | tf_op jit(solution)/shard_map/scatter | solution.py:63
  35.0 11.1 %all-to-all-start = ((s32[128,1,8]{2,1,0:T(1,128)}), s32[128,1,8]{2,1,0:T(1,128)S(1)}, u32[]{:S(2)}, u32[]{:S(2)}) async-start(s32[128,1,8]{2,1,0:T(1,128)} %copy.29), calls=%async_computation | async-start | bytes 131072 | tf_op jit(solution)/shard_map/all_to_all | solution.py:65
  46.2 8.3 convolution_convert_fusion.1
  56.0 8.8 gather_fusion
  67.9 9.1 all-to-all-start.1
  81.5 22.1 %collective-permute-done = f32[16,32]{1,0:T(8,128)S(1)} collective-permute-done((f32[16,32]{1,0:T(8,128)S(1)}, f32[16,32]{1,0:T(8,128)S(1)}, u32[]{:S(2)}, u32[]{:S(2)}) %collective-permute-start) | collective-permute-done | bytes 2080 | tf_op jit(solution)/shard_map/ppermute | solution.py:19
  103.5 5.3 collective-permute-start.3
  110.5 5.3 collective-permute-start.5
  117.5 5.3 collective-permute-start.7
  124.5 5.3 collective-permute-start.9
  131.4 5.3 collective-permute-start.11
  138.4 5.3 collective-permute-start.13
  152.9 7.7 gather_fusion.1
  161.0 20.9 %all-gather = f32[16,32,16]{1,2,0:T(8,128)S(1)} all-gather(f32[1,32,16]{1,2,0:T(8,128)S(1)} %get-tuple-element.28), channel_id=1, replica_groups=mesh['group'=8,'pair'=16] {'pair'}, dimensions={0}, use_global_device_ids=true | all-gather | bytes 34816 | tf_op jit(solution)/shard_map/all_gather | solution.py:77
  182.7 23.8 %all-gather.1 = f32[16,32,16]{1,2,0:T(8,128)S(1)} all-gather(f32[1,32,16]{1,2,0:T(8,128)S(1)} %multiply_bitcast_fusion), channel_id=1, replica_groups=mesh['group'=8,'pair'=16] {'pair'}, dimensions={0}, use_global_device_ids=true | all-gather | bytes 34816 | tf_op jit(solution)/shard_map/all_gather | solution.py:86
  210.2 73.0 %scatter_fusion.1 = bf16[128,8,1024]{2,1,0:T(8,128)(2,1)} fusion(bf16[128,8,1024]{2,1,0:T(8,128)(2,1)} %broadcast_in_dim.23, s32[512]{0:T(512)S(1)} %bitcast.82, bf16[512,1024]{1,0:T(8,128)(2,1)} %fusion.5), kind=kCustom, calls=%fused_computation.3 | custom fusion | bytes 3149824 | tf_op jit(solution)/shard_map/scatter | solution.py:105
  283.2 8.1 all-to-all-start.2
  292.4 28.1 %all-to-all-done.2 = bf16[128,8,1024]{2,1,0:T(8,128)(2,1)} async-done(((bf16[128,8,1024]{2,1,0:T(8,128)(2,1)}), bf16[128,8,1024]{2,1,0:T(8,128)(2,1)}, u32[]{:S(2)}, u32[]{:S(2)}) %all-to-all-start.2) | async-done | bytes 2097184 | tf_op jit(solution)/shard_map/all_to_all | solution.py:107
  320.5 13.4 %scatter_custom_fusion.2 = f32[2048,1024]{1,0:T(8,128)} fusion(s32[1024]{0:T(1024)S(1)} %bitcast.102, f32[]{:T(128)} %constant.174.clone.1, bf16[128,8,1024]{2,1,0:T(8,128)(2,1)} %all-to-all-done.2), kind=kCustom, calls=%fused_computation.5 | custom fusion | flops 2097152 | bytes 10485764 | tf_op jit(solution)/shard_map/scatter-add | solution.py:111
  333.9 11.2 %convolution_bitcast_fusion = f32[1024,1024]{0,1:T(8,128)} fusion(bf16[2048,1024]{1,0:T(8,128)(2,1)} %param.10, f32[2048,1024]{1,0:T(8,128)} %scatter_custom_fusion.2), kind=kOutput, calls=%fused_computation.10 | convolution fusion | flops 4297064448 | bytes 16777216 | tf_op jit(solution)/shard_map/pr,pe->re/dot_general | solution.py:118
  345.1 5.3 copy.37
  351.6 72.1 %all-reduce.2 = (bf16[16]{0:T(256)(128)(2,1)S(1)}, bf16[16,1024]{1,0:T(8,128)(2,1)S(1)}) all-reduce(bf16[16]{0:T(256)(128)(2,1)S(1)} %multiply_convert_fusion.1, bf16[16,1024]{1,0:T(8,128)(2,1)S(1)} %multiply_convert_fusion), channel_id=2, replica_groups=mesh['group'=8,'pair'=16] {'pair'}, use_global_device_ids=true, to_apply=%region_7.8.clone | all-reduce | flops 16400 | bytes 65600
  426.9 9.5 convolution_convert_fusion
  436.4 554.0 %reduce-scatter.4.cloned.1.call-done = f32[8,1024]{1,0:T(8,128)} async-done(((f32[1024,1024]{1,0:T(8,128)}), f32[8,1024]{1,0:T(8,128)}) %reduce-scatter.4.cloned.1.call-update) | async-done | bytes 32784
  (102 shorter events, 41.8 us)
Async XLA Ops:
  7.2 39.0 %copy-start = (bf16[1024,1024]{1,0:T(8,128)(2,1)S(1)}, bf16[1024,1024]{1,0:T(8,128)(2,1)}, u32[]{:S(2)}) copy-start(bf16[1024,1024]{1,0:T(8,128)(2,1)} %param.11) | copy-start | bytes 6291460
  35.0 20.6 %all-to-all-start = ((s32[128,1,8]{2,1,0:T(1,128)}), s32[128,1,8]{2,1,0:T(1,128)S(1)}, u32[]{:S(2)}, u32[]{:S(2)}) async-start(s32[128,1,8]{2,1,0:T(1,128)} %copy.29), calls=%async_computation | async-start | bytes 131072 | tf_op jit(solution)/shard_map/all_to_all | solution.py:65
  64.7 12.3 %copy-start.2 = (f32[1,1,16,32]{3,2,1,0:T(8,128)S(1)}, f32[1,1,16,32]{3,2,1,0:T(8,128)}, u32[]{:S(2)}) copy-start(f32[1,1,16,32]{3,2,1,0:T(8,128)} %param.7) | copy-start | bytes 6148
  64.7 16.7 %copy-start.1 = (bf16[1,16,1024]{2,1,0:T(8,128)(2,1)S(1)}, bf16[1,16,1024]{2,1,0:T(8,128)(2,1)}, u32[]{:S(2)}) copy-start(bf16[1,16,1024]{2,1,0:T(8,128)(2,1)} %param.6) | copy-start | bytes 98308
  67.9 85.0 %all-to-all-start.1 = ((bf16[128,8,1024]{2,1,0:T(8,128)(2,1)}), bf16[128,8,1024]{2,1,0:T(8,128)(2,1)}, u32[]{:S(2)}, u32[]{:S(2)}) async-start(bf16[128,8,1024]{2,1,0:T(8,128)(2,1)} %bitcast_select_fusion), calls=%async_computation.1 | async-start | bytes 4194304 | tf_op jit(solution)/shard_map/all_to_all | solution.py:69
  77.1 26.5 %collective-permute-start.1 = (f32[16,32]{1,0:T(8,128)S(1)}, f32[16,32]{1,0:T(8,128)S(1)}, u32[]{:S(2)}, u32[]{:S(2)}) collective-permute-start(f32[16,32]{1,0:T(8,128)S(1)} %bitcast.98), channel_id=1, source_target_pairs={{0,15},{1,0},{2,1},{3,2},{4,3},{5,4},{6,5},{7,6},{8,7},{9,8},{10,9... | collective-permute-start | bytes 6152 | tf_op jit(solution)/shard_map/ppermute | solution.py:24
  81.4 22.1 %collective-permute-start = (f32[16,32]{1,0:T(8,128)S(1)}, f32[16,32]{1,0:T(8,128)S(1)}, u32[]{:S(2)}, u32[]{:S(2)}) collective-permute-start(f32[16,32]{1,0:T(8,128)S(1)} %bitcast.99), channel_id=1, source_target_pairs={{0,1},{1,2},{2,3},{3,4},{4,5},{5,6},{6,7},{7,8},{8,9},{9,10},{10,1... | collective-permute-start | bytes 6152 | tf_op jit(solution)/shard_map/ppermute | solution.py:19
  103.5 7.0 collective-permute-start.2
  103.5 7.0 collective-permute-start.3
  110.5 7.0 collective-permute-start.4
  110.5 7.0 collective-permute-start.5
  117.5 7.0 collective-permute-start.6
  117.5 7.0 collective-permute-start.7
  124.5 7.0 collective-permute-start.8
  124.5 7.0 collective-permute-start.9
  131.4 7.0 collective-permute-start.10
  131.4 7.0 collective-permute-start.11
  138.4 7.0 collective-permute-start.12
  138.4 11.1 %collective-permute-start.13 = (f32[16,32]{1,0:T(8,128)S(1)}, f32[16,32]{1,0:T(8,128)S(1)}, u32[]{:S(2)}, u32[]{:S(2)}) collective-permute-start(f32[16,32]{1,0:T(8,128)S(1)} %collective-permute-done.11), channel_id=1, source_target_pairs={{0,15},{1,0},{2,1},{3,2},{4,3},{5,4},{6,5},{7,6},{8,7},{9,8},{10,9... | collective-permute-start | bytes 6152 | tf_op jit(solution)/shard_map/ppermute | solution.py:24
  145.4 7.0 collective-permute-start.14
  283.2 37.4 %all-to-all-start.2 = ((bf16[128,8,1024]{2,1,0:T(8,128)(2,1)}), bf16[128,8,1024]{2,1,0:T(8,128)(2,1)}, u32[]{:S(2)}, u32[]{:S(2)}) async-start(bf16[128,8,1024]{2,1,0:T(8,128)(2,1)} %scatter_fusion.1), calls=%async_computation.2 | async-start | bytes 4194304 | tf_op jit(solution)/shard_map/all_to_all | solution.py:107
  291.3 699.1 %reduce-scatter.4.cloned.1.call-start = ((), (), s32[]{:S(2)}) async-start(), calls=%async_computation.4 | async-start | bytes 4227072
  350.4 0.7 copy-start.3
Sparse Core Ops, SparseCore 0:
  350.6 639.7 reduce-scatter.3
